TPU v7x, 256 devices: a whole 4x4x8 slice. The times are simulated.
256 devices in a mesh: row: 8 (over x, core), col: 16 (over y, z_hi), rep: 2 (over z_lo).
Axes of the slice: x: 4, y: 4, z: 8 (z_hi: 4, z_lo: 2; z = z_hi * 2 + z_lo), core: 2. Of those that a mesh axis runs over, the one named last changes fastest.
Arguments:
- slab_half: float32 [2, 8192, 4096], P('rep', 'row', 'col'), may hold values from -6 to 6
- window_half: float32 [2, 4096, 8192], P('rep', 'row', 'col'), may hold values from -0.125 to 0.125
- slab_cols: int32 [64, 20], replicated, may hold values from 0 to 63, as said below
- window_cols: int32 [64, 20], replicated, may hold values from 0 to 63, as said below
Outputs:
- slab_square: float32 [8192, 8192], P(('row', 'rep'), 'col')
Inputs may be any that keep to these rules, and one draw needn't show every extreme that they name: `slab_cols`: each slab block row i lists 20 distinct block columns, all within 24 blocks of its centre, block column i; it lists the column exactly 24 blocks above the centre where that column exists, else the one exactly 24 blocks below where that exists. `window_cols`: each window block row k lists 20 distinct block columns, all within 24 blocks of column k; it lists column k + 24 where that column exists, else column k - 24 where that exists.
All inputs are finite; a program needn't handle non-finite values.
Results may differ from a plain program's by a relative error of at most 0.0001.
Values sent between devices are 32-bit elements; how exact they have to be, the bound alone decides.
A program may use at most 128 MiB of HBM per device.

v0:
```python
import jax
import jax.numpy as jnp
from jax import lax
from jax.sharding import PartitionSpec as P

BS = 128


def block_mask(columns, width):
    hit = columns[:, :, None] == jnp.arange(width, dtype=jnp.int32)[None, None, :]
    return jnp.any(hit, axis=1)


def expand(mask, size):
    filled = mask.astype(jnp.float32)
    return jnp.repeat(jnp.repeat(filled, size, axis=0), size, axis=1)


def product(left, right):
    return jnp.dot(left, right, precision=lax.Precision.HIGHEST, preferred_element_type=jnp.float32)


def body(slab_half, window_half, slab_cols, window_cols):
    row_index = lax.axis_index("row")
    col_index = lax.axis_index("col")
    rep_index = lax.axis_index("rep")
    window_width = window_cols.shape[0]
    half_blocks = window_width // lax.axis_size("rep")
    slab_blocks = half_blocks // lax.axis_size("col")
    window_blocks = half_blocks // lax.axis_size("row")
    slab_local = slab_half[0]
    window_local = window_half[0]
    row_blocks = slab_local.shape[0] // BS
    col_blocks = window_local.shape[1] // BS
    mask_a = block_mask(slab_cols, window_width)
    mask_b = block_mask(window_cols, window_width)
    half_start = rep_index * half_blocks
    row_start = row_index * row_blocks
    col_start = col_index * col_blocks
    mine_a = lax.dynamic_slice(
        mask_a, (row_start, half_start + col_index * slab_blocks), (row_blocks, slab_blocks)
    )
    mine_b = lax.dynamic_slice(
        mask_b, (half_start + row_index * window_blocks, col_start), (window_blocks, col_blocks)
    )
    slab_kept = slab_local * expand(mine_a, BS)
    window_kept = window_local * expand(mine_b, BS)
    slab_whole = lax.all_gather(slab_kept, "col", axis=1, tiled=True)
    partial_sum = product(slab_whole, lax.all_gather(window_kept, "row", axis=0, tiled=True))
    reduced = lax.psum_scatter(partial_sum, "rep", scatter_dimension=0, tiled=True)
    out_mask = expand(
        lax.dynamic_slice(mask_a, (row_start, col_start), (row_blocks, col_blocks)), BS
    )
    share = reduced.shape[0]
    out_local = lax.dynamic_slice_in_dim(out_mask, rep_index * share, share, 0)
    return reduced * out_local


def solution(mesh):
    in_specs = (P("rep", "row", "col"), P("rep", "row", "col"), P(), P())
    out_specs = P(("row", "rep"), "col")
    return jax.shard_map(body, mesh=mesh, in_specs=in_specs, out_specs=out_specs, check_vma=False)
```

profile of v0, /device:TPU:1, one launch (start us, length us, event | category | flops | bytes accessed | tf_op | source)
XLA Modules:
  0.0 355.2 jit_solution(626893484085413982)
XLA Ops:
  6.5 0.0 copy-start
  6.5 0.0 all-gather.5.cloned.1.call-start
  6.5 1.0 fusion.1
  7.6 0.1 dynamic-slice_convert_fusion.2
  7.7 0.6 broadcast_in_dim.25
  8.3 2.5 bitcast_multiply_fusion
  10.8 0.0 all-gather.5.cloned.1.call-update
  10.8 0.0 all-gather.3.cloned.1.call-start
  10.9 0.9 fusion
  11.8 0.1 dynamic-slice_convert_fusion.1
  11.9 1.2 broadcast_in_dim.23
  13.2 0.0 copy-done
  13.2 1.1 bitcast_multiply_fusion.1
  14.3 0.0 all-gather.3.cloned.1.call-update
  14.3 0.0 reduce-scatter.2.cloned.1.call-start
  14.4 53.0 %all-gather.5.cloned.1.call-done = f32[4096,512]{1,0:T(8,128)} async-done(((f32[512,512]{1,0:T(8,128)}), f32[4096,512]{1,0:T(8,128)}) %all-gather.5.cloned.1.call-update) | async-done | bytes 8388624 | tf_op jit(solution)/shard_map/all_gather | solution.py:49
  67.3 211.3 %all-gather.3.cloned.1.call-done = f32[1024,4096]{1,0:T(8,128)} async-done(((f32[1024,256]{1,0:T(8,128)}), f32[1024,4096]{1,0:T(8,128)}) %all-gather.3.cloned.1.call-update) | async-done | bytes 16777232 | tf_op jit(solution)/shard_map/all_gather | solution.py:48
  278.6 31.0 %fusion.2 = f32[1024,512]{1,0:T(8,128)} fusion(f32[1024,4096]{1,0:T(8,128)} %all-gather.3.cloned.1.call-done, f32[4096,512]{1,0:T(8,128)} %all-gather.5.cloned.1.call-done), kind=kOutput, calls=%fused_computation.11 | convolution fusion | flops 25769803776 | bytes 27262976 | tf_op jit(solution)/shard_map/dot_general | solution.py:20
  309.6 0.0 reduce-scatter.2.cloned.1.call-update
  309.7 0.1 dynamic-slice_convert_fusion
  309.8 1.2 broadcast_in_dim.27
  311.0 0.2 copy.13
  311.2 35.1 %reduce-scatter.2.cloned.1.call-done = f32[512,512]{1,0:T(8,128)} async-done(((f32[1024,512]{1,0:T(8,128)}), f32[512,512]{1,0:T(8,128)}) %reduce-scatter.2.cloned.1.call-update) | async-done | bytes 1048592 | tf_op jit(solution)/shard_map/reduce_scatter | solution.py:50
  346.3 2.4 dynamic-slice_multiply_fusion
  (3 shorter events, 0.1 us)
Async XLA Ops:
  6.5 6.6 %copy-start = (f32[1,1024,256]{2,1,0:T(8,128)S(1)}, f32[1,1024,256]{2,1,0:T(8,128)}, u32[]{:S(2)}) copy-start(f32[1,1024,256]{2,1,0:T(8,128)} %param.4) | copy-start | bytes 3145732
  6.5 60.8 %all-gather.5.cloned.1.call-start = ((), (), s32[]{:S(2)}) async-start(), calls=%async_computation.2 | async-start | bytes 9437184 | tf_op jit(solution)/shard_map/all_gather | solution.py:49
  10.8 267.8 %all-gather.3.cloned.1.call-start = ((), (), s32[]{:S(2)}) async-start(), calls=%async_computation.1 | async-start | bytes 17825792 | tf_op jit(solution)/shard_map/all_gather | solution.py:48
  14.3 332.0 %reduce-scatter.2.cloned.1.call-start = ((), (), s32[]{:S(2)}) async-start(), calls=%async_computation.3 | async-start | bytes 3145728 | tf_op jit(solution)/shard_map/reduce_scatter | solution.py:50
Sparse Core Ops, SparseCore 0:
  10.9 56.3 all-gather.4
  69.7 208.8 all-gather.2
  309.8 36.4 reduce-scatter.1
where the time goes:
time: 355 us
  waiting for transfers between devices  299 us (84%)
  matrix products  31 us (9%)
  between operations  13.2 us (4%)
  other arithmetic  8.21 us (2%)
    all_gather x1, waiting for transfers between devices, body(): slab_whole = lax.all_gather(slab_kept, 'col', axis=1, tiled=True)  211 us
    all_gather x1, waiting for transfers between devices, body(): lax.all_gather(window_kept, 'row', axis=0, tiled=True)  53 us
    reduce_scatter x1, waiting for transfers between devices, body(): lax.psum_scatter(partial_sum, 'rep', scatter_dimension=0, tiled=True)  35.1 us
    dot_general x1, matrix products, product(): jnp.dot(left, right, precision=lax.Precision.HIGHEST, preferred_element_t...  31 us
  transfers between devices with their start and end apart: 3, of which 3 were waited for; matrix products, arithmetic and copies ran while one was open for 1% of the time, Pallas kernels for 0%

commit v1 on v0

--- a/solution.py
+++ b/solution.py
@@ -45,7 +45,9 @@
     )
     slab_kept = slab_local * expand(mine_a, BS)
     window_kept = window_local * expand(mine_b, BS)
-    slab_whole = lax.all_gather(slab_kept, "col", axis=1, tiled=True)
+    slab_whole = jnp.concatenate(
+        lax.all_to_all(jnp.stack([slab_kept] * lax.axis_size("col")), "col", 0, 0), axis=1
+    )
     partial_sum = product(slab_whole, lax.all_gather(window_kept, "row", axis=0, tiled=True))
     reduced = lax.psum_scatter(partial_sum, "rep", scatter_dimension=0, tiled=True)
     out_mask = expand(

time: 355 us -> 508 us (1.43)
  waiting for transfers between devices: 299 us -> 432 us
  starting transfers between devices: 0.09 us -> 12.2 us
  local copies, waits for them, and re-layouts: 3.34 us -> 12.4 us
    all_to_all x0 -> x1, waiting for transfers between devices: none -> 312 us  [body(): lax.all_to_all(jnp.stack([slab_kept] * lax.axis_size('col')), 'col', 0, 0)]
    all_gather x1 -> x0, waiting for transfers between devices: 211 us -> none  [body(): slab_whole = lax.all_gather(slab_kept, 'col', axis=1, tiled=True)]
    reduce_scatter x1, waiting for transfers between devices: 35.1 us -> 66.3 us  [body(): lax.psum_scatter(partial_sum, 'rep', scatter_dimension=0, tiled=True)]
    all_to_all x0 -> x1, starting transfers between devices: none -> 11.9 us  [body(): lax.all_to_all(jnp.stack([slab_kept] * lax.axis_size('col')), 'col', 0, 0)]
    another operation x0 -> x2, local copies, waits for them, and re-layouts: none -> 8.18 us  [body(): jnp.stack([slab_kept] * lax.axis_size('col'))]
where the time goes in v1:
time: 508 us
  waiting for transfers between devices  432 us (85%)
  matrix products  31 us (6%)
  between operations  13.5 us (3%)
  local copies, waits for them, and re-layouts  12.4 us (2%)
  starting transfers between devices  12.2 us (2%)
  other arithmetic  6.47 us (1%)
    all_to_all x1, waiting for transfers between devices, body(): lax.all_to_all(jnp.stack([slab_kept] * lax.axis_size('col')), 'col', 0, 0)  312 us
    reduce_scatter x1, waiting for transfers between devices, body(): lax.psum_scatter(partial_sum, 'rep', scatter_dimension=0, tiled=True)  66.3 us
    all_gather x1, waiting for transfers between devices, body(): lax.all_gather(window_kept, 'row', axis=0, tiled=True)  54.4 us
    dot_general x1, matrix products, product(): jnp.dot(left, right, precision=lax.Precision.HIGHEST, preferred_element_t...  31 us
    all_to_all x1, starting transfers between devices, body(): lax.all_to_all(jnp.stack([slab_kept] * lax.axis_size('col')), 'col', 0, 0)  11.9 us
  transfers between devices with their start and end apart: 3, of which 3 were waited for; matrix products, arithmetic and copies ran while one was open for 1% of the time, Pallas kernels for 0%

profile of v1, /device:TPU:1, one launch (start us, length us, event | category | flops | bytes accessed | tf_op | source)
XLA Modules:
  0.0 507.9 jit_solution(10420544251533056419)
XLA Ops:
  6.5 0.9 fusion
  7.5 0.1 dynamic-slice_convert_fusion.1
  7.6 1.2 broadcast_in_dim.23
  8.9 0.8 reshape.29
  9.7 1.4 multiply_bitcast_fusion
  11.1 0.3 copy.10
  11.5 7.8 %stack.5 = f32[16,1024,256]{1,2,0:T(8,128)} broadcast(f32[1024,256]{0,1:T(8,128)S(1)} %copy.10), dimensions={1,2} | broadcast | bytes 17825792 | tf_op jit(solution)/shard_map/stack | solution.py:49
  19.3 0.0 copy-start.1
  19.3 0.0 copy-start
  19.3 11.9 %all-to-all-start = ((f32[16,1024,256]{1,2,0:T(8,128)}), f32[16,1024,256]{1,2,0:T(8,128)}, u32[]{:S(2)}, u32[]{:S(2)}) async-start(f32[16,1024,256]{1,2,0:T(8,128)} %stack.5), calls=%async_computation | async-start | bytes 33554432 | tf_op jit(solution)/shard_map/all_to_all | solution.py:49
  31.3 0.0 all-gather.2.cloned.1.call-start
  31.3 0.0 copy-done.1
  31.3 0.2 fusion.1
  31.6 0.1 dynamic-slice_convert_fusion.2
  31.7 0.6 broadcast_in_dim.25
  32.3 0.0 copy-done
  32.3 1.2 bitcast_multiply_fusion
  33.5 0.0 all-gather.2.cloned.1.call-update
  33.5 0.2 reduce-scatter.2.cloned.1.call-start
  33.7 54.4 %all-gather.2.cloned.1.call-done = f32[4096,512]{1,0:T(8,128)} async-done(((f32[512,512]{1,0:T(8,128)}), f32[4096,512]{1,0:T(8,128)}) %all-gather.2.cloned.1.call-update) | async-done | bytes 8388624 | tf_op jit(solution)/shard_map/all_gather | solution.py:51
  88.2 311.5 %all-to-all-done = f32[16,1024,256]{1,2,0:T(8,128)} async-done(((f32[16,1024,256]{1,2,0:T(8,128)}), f32[16,1024,256]{1,2,0:T(8,128)}, u32[]{:S(2)}, u32[]{:S(2)}) %all-to-all-start) | async-done | bytes 16777248 | tf_op jit(solution)/shard_map/all_to_all | solution.py:49
  399.7 31.0 %fusion.2 = f32[1024,512]{1,0:T(8,128)} fusion(f32[1024,4096]{0,1:T(8,128)} %bitcast.3, f32[4096,512]{1,0:T(8,128)} %all-gather.2.cloned.1.call-done), kind=kOutput, calls=%fused_computation.11 | convolution fusion | flops 25769803776 | bytes 27262976 | tf_op jit(solution)/shard_map/dot_general | solution.py:20
  430.7 0.0 reduce-scatter.2.cloned.1.call-update
  430.8 0.1 dynamic-slice_convert_fusion
  430.9 1.2 broadcast_in_dim.27
  432.1 0.2 copy.15
  432.3 66.3 %reduce-scatter.2.cloned.1.call-done = f32[512,512]{1,0:T(8,128)} async-done(((f32[1024,512]{1,0:T(8,128)}), f32[512,512]{1,0:T(8,128)}) %reduce-scatter.2.cloned.1.call-update) | async-done | bytes 1048592 | tf_op jit(solution)/shard_map/reduce_scatter | solution.py:52
  498.6 2.4 dynamic-slice_multiply_fusion
  (3 shorter events, 0.1 us)
Async XLA Ops:
  19.3 12.0 %copy-start.1 = (s32[64,20]{0,1:T(8,128)S(1)}, s32[64,20]{0,1:T(8,128)}, u32[]{:S(2)}) copy-start(s32[64,20]{0,1:T(8,128)} %param.7) | copy-start | bytes 15364
  19.3 13.0 %copy-start = (f32[1,512,512]{2,1,0:T(8,128)S(1)}, f32[1,512,512]{2,1,0:T(8,128)}, u32[]{:S(2)}) copy-start(f32[1,512,512]{2,1,0:T(8,128)} %param.5) | copy-start | bytes 3145732
  19.3 380.4 %all-to-all-start = ((f32[16,1024,256]{1,2,0:T(8,128)}), f32[16,1024,256]{1,2,0:T(8,128)}, u32[]{:S(2)}, u32[]{:S(2)}) async-start(f32[16,1024,256]{1,2,0:T(8,128)} %stack.5), calls=%async_computation | async-start | bytes 33554432 | tf_op jit(solution)/shard_map/all_to_all | solution.py:49
  31.3 56.9 %all-gather.2.cloned.1.call-start = ((), (), s32[]{:S(2)}) async-start(), calls=%async_computation.2 | async-start | bytes 9437184 | tf_op jit(solution)/shard_map/all_gather | solution.py:51
  33.5 465.2 %reduce-scatter.2.cloned.1.call-start = ((), (), s32[]{:S(2)}) async-start(), calls=%async_computation.3 | async-start | bytes 3145728 | tf_op jit(solution)/shard_map/reduce_scatter | solution.py:52
Sparse Core Ops, SparseCore 0:
  33.9 54.1 all-gather.1
  430.9 67.7 reduce-scatter.1
